TPU v7x, 512 devices: a whole 4x8x8 slice. The times are simulated.
512 devices in a mesh: ctx: 32 (over z, x), head: 16 (over y, core).
Axes of the slice: x: 4, y: 8, z: 8, core: 2. Of those that a mesh axis runs over, the one named last changes fastest.
Arguments:
- queries: bfloat16 [16384, 4096], P(('ctx', 'head')), may hold values from -64 to 64
- keys: bfloat16 [16384, 4096], P(('ctx', 'head')), may hold values from -8 to 8
- values: bfloat16 [16384, 4096], P(('ctx', 'head')), may hold values from -6 to 6
Outputs:
- attended: bfloat16 [16384, 4096], P(('ctx', 'head'))
All inputs are finite; a program needn't handle non-finite values.
Results may differ from a plain program's by a relative error of at most 0.0045.
Values may be sent and summed in bfloat16 or wider, within the bound.
No kernel may reach another device: no remote copies, remote signals or barrier semaphores. Data moves between devices by JAX's collectives and lax.ppermute only.
A program may use at most 64 MiB of HBM per device.

v0:
```python
import jax
import jax.numpy as jnp
from jax import lax
from jax.sharding import PartitionSpec as P

HEAD_SIZE = 128
BLOCK = 256
SUM = 16
BAND_REACH = 1024


def from_behind(value, axis, steps):
    count = lax.axis_size(axis)
    initial, last = (max(0, -steps), min(count, count - steps))
    return lax.ppermute(value, axis, [(source, source + steps) for source in range(initial, last)])


def summary_positions(count):
    ridx = jnp.arange(count, dtype=jnp.int32)
    return ridx // SUM * BLOCK + BLOCK - SUM + ridx % SUM


def band_scores(qblk, kb, qpos, bpos):
    scores = jnp.einsum(
        "qhd,khd->hqk", qblk, kb, preferred_element_type=jnp.float32
    ) * HEAD_SIZE ** (-0.5)
    diff = qpos[:, None] - bpos[None, :]
    band_ok = (bpos[None, :] >= 0) & (diff >= 0) & (diff < BAND_REACH)
    return (jnp.where(band_ok[None], scores, -1e30), band_ok)


def sum_scores(qblk, ks, qpos, spos):
    scores = jnp.einsum(
        "qhd,khd->hqk", qblk, ks, preferred_element_type=jnp.float32
    ) * HEAD_SIZE ** (-0.5)
    sum_ok = qpos[:, None] - spos[None, :] >= BAND_REACH
    return (jnp.where(sum_ok[None], scores, -1e30), sum_ok)


def local(queries, keys, values):
    q_dev, k_dev, v_dev = (
        lax.all_to_all(queries, "head", split_axis=1, concat_axis=0, tiled=True),
        lax.all_to_all(keys, "head", split_axis=1, concat_axis=0, tiled=True),
        lax.all_to_all(values, "head", split_axis=1, concat_axis=0, tiled=True),
    )
    tok_rows = q_dev.shape[0]
    heads_here = q_dev.shape[1] // HEAD_SIZE
    q_all = q_dev.reshape(tok_rows, heads_here, HEAD_SIZE)
    k_all = k_dev.reshape(tok_rows, heads_here, HEAD_SIZE)
    value_rows_all = v_dev.reshape(tok_rows, heads_here, HEAD_SIZE)
    base = lax.axis_index("ctx") * tok_rows
    reach_devs = (BAND_REACH + tok_rows - 1) // tok_rows
    band_k_parts = []
    band_v_parts = []
    for dist in range(reach_devs, 0, -1):
        prev_k, prev_v = from_behind((k_all, value_rows_all), "ctx", dist)
        band_k_parts.append(prev_k)
        band_v_parts.append(prev_v)
    k_band = jnp.concatenate(band_k_parts + [k_all], axis=0)
    v_band = jnp.concatenate(band_v_parts + [value_rows_all], axis=0)
    k_sum = k_all.reshape(tok_rows // BLOCK, BLOCK, heads_here, HEAD_SIZE)[
        :, BLOCK - SUM :
    ].reshape(-1, heads_here, HEAD_SIZE)
    v_sum = value_rows_all.reshape(tok_rows // BLOCK, BLOCK, heads_here, HEAD_SIZE)[
        :, BLOCK - SUM :
    ].reshape(-1, heads_here, HEAD_SIZE)
    query_rows = min(512, tok_rows)
    k_seen, v_seen = (
        lax.all_gather(k_sum, "ctx", axis=0, tiled=True),
        lax.all_gather(v_sum, "ctx", axis=0, tiled=True),
    )
    spos = summary_positions(k_seen.shape[0])
    qpos = base + 0 + jnp.arange(query_rows, dtype=jnp.int32)
    bpos = base + 0 - BAND_REACH + jnp.arange(BAND_REACH + query_rows, dtype=jnp.int32)
    sb, band_ok = band_scores(q_all, k_band, qpos, bpos)
    ss, sum_ok = sum_scores(q_all, k_seen, qpos, spos)
    top = jnp.maximum(jnp.max(sb, axis=-1), jnp.max(ss, axis=-1))
    pb = jnp.where(band_ok[None], jnp.exp(sb - top[..., None]), 0.0)
    ps = jnp.where(sum_ok[None], jnp.exp(ss - top[..., None]), 0.0)
    total = jnp.sum(pb, axis=-1) + jnp.sum(ps, axis=-1)
    numer = jnp.einsum(
        "hqk,khd->hqd", pb.astype(jnp.bfloat16), v_band, preferred_element_type=jnp.float32
    )
    numer = numer + jnp.einsum(
        "hqk,khd->hqd", ps.astype(jnp.bfloat16), v_seen, preferred_element_type=jnp.float32
    )
    outputs = (numer / total[..., None]).astype(jnp.bfloat16)
    local_out = jnp.transpose(outputs, (1, 0, 2)).reshape(tok_rows, heads_here * HEAD_SIZE)
    return lax.all_to_all(local_out, "head", split_axis=0, concat_axis=1, tiled=True)


def solution(mesh):
    placed = (P(("ctx", "head"), None), P(("ctx", "head"), None), P(("ctx", "head"), None))
    return jax.shard_map(
        local, mesh=mesh, in_specs=placed, out_specs=P(("ctx", "head"), None), check_vma=False
    )
```

profile of v0, /device:TPU:1, one launch (start us, length us, event | category | flops | bytes accessed | tf_op | source)
XLA Modules:
  0.0 202.9 jit_solution(5113818668140750158)
XLA Ops:
  0.0 1.7 copy.54
  1.7 10.2 %all-to-all-start = ((bf16[32,16,256]{2,0,1:T(8,128)(2,1)}), bf16[32,16,256]{2,0,1:T(8,128)(2,1)S(1)}, u32[]{:S(2)}, u32[]{:S(2)}) async-start(bf16[32,16,256]{2,0,1:T(8,128)(2,1)} %bitcast.48), calls=%async_computation | async-start | bytes 524288 | tf_op jit(solution)/shard_map/all_to_all | solution.py:43
  11.9 1.7 copy.52
  13.5 10.2 %all-to-all-done = bf16[32,16,256]{2,0,1:T(8,128)(2,1)S(1)} async-done(((bf16[32,16,256]{2,0,1:T(8,128)(2,1)}), bf16[32,16,256]{2,0,1:T(8,128)(2,1)S(1)}, u32[]{:S(2)}, u32[]{:S(2)}) %all-to-all-start) | async-done | bytes 262176 | tf_op jit(solution)/shard_map/all_to_all | solution.py:43
  23.7 3.4 %all-to-all-start.2 = ((bf16[32,16,256]{2,0,1:T(8,128)(2,1)}), bf16[32,16,256]{2,0,1:T(8,128)(2,1)S(1)}, u32[]{:S(2)}, u32[]{:S(2)}) async-start(bf16[32,16,256]{2,0,1:T(8,128)(2,1)} %bitcast.46), calls=%async_computation.2 | async-start | bytes 524288 | tf_op jit(solution)/shard_map/all_to_all | solution.py:44
  27.2 1.7 copy.53
  28.9 0.4 subtract_compare_fusion.2
  29.3 8.9 %all-to-all-done.2 = bf16[32,16,256]{2,0,1:T(8,128)(2,1)S(1)} async-done(((bf16[32,16,256]{2,0,1:T(8,128)(2,1)}), bf16[32,16,256]{2,0,1:T(8,128)(2,1)S(1)}, u32[]{:S(2)}, u32[]{:S(2)}) %all-to-all-start.2) | async-done | bytes 262176 | tf_op jit(solution)/shard_map/all_to_all | solution.py:44
  38.2 3.4 %all-to-all-start.1 = ((bf16[32,16,256]{2,0,1:T(8,128)(2,1)}), bf16[32,16,256]{2,0,1:T(8,128)(2,1)S(1)}, u32[]{:S(2)}, u32[]{:S(2)}) async-start(bf16[32,16,256]{2,0,1:T(8,128)(2,1)} %bitcast.47), calls=%async_computation.1 | async-start | bytes 524288 | tf_op jit(solution)/shard_map/all_to_all | solution.py:42
  41.6 1.3 fusion.7
  42.9 0.1 reshape.152
  43.0 3.7 %collective-permute-start = (bf16[512,2,128]{2,0,1:T(8,128)(2,1)S(1)}, bf16[512,2,128]{2,0,1:T(8,128)(2,1)}, u32[]{:S(2)}, u32[]{:S(2)}) collective-permute-start(bf16[512,2,128]{2,0,1:T(8,128)(2,1)S(1)} %copy.21), channel_id=1, source_target_pairs={{0,32},{16,48},{32,64},{48,80},{64,96},{80,112},{96,128},{112,144}... | collective-permute-start | bytes 786440 | tf_op jit(solution)/shard_map/ppermute | solution.py:15
  46.7 2.9 %collective-permute-start.1 = (bf16[512,2,128]{2,0,1:T(8,128)(2,1)S(1)}, bf16[512,2,128]{2,0,1:T(8,128)(2,1)}, u32[]{:S(2)}, u32[]{:S(2)}) collective-permute-start(bf16[512,2,128]{2,0,1:T(8,128)(2,1)S(1)} %copy.21), channel_id=1, source_target_pairs={{0,16},{16,32},{32,48},{48,64},{64,80},{80,96},{96,112},{112,128},... | collective-permute-start | bytes 786440 | tf_op jit(solution)/shard_map/ppermute | solution.py:15
  49.7 0.1 reshape_reshape.6
  49.7 0.1 reshape_reshape.7
  49.8 0.1 reshape.155
  49.9 4.8 %collective-permute-start.2 = (bf16[512,2,128]{2,0,1:T(8,128)(2,1)S(1)}, bf16[512,2,128]{2,0,1:T(8,128)(2,1)}, u32[]{:S(2)}, u32[]{:S(2)}) collective-permute-start(bf16[512,2,128]{2,0,1:T(8,128)(2,1)S(1)} %copy.29), channel_id=1, source_target_pairs={{0,32},{16,48},{32,64},{48,80},{64,96},{80,112},{96,128},{112,144}... | collective-permute-start | bytes 786440 | tf_op jit(solution)/shard_map/ppermute | solution.py:15
  54.7 3.8 %collective-permute-start.3 = (bf16[512,2,128]{2,0,1:T(8,128)(2,1)S(1)}, bf16[512,2,128]{2,0,1:T(8,128)(2,1)}, u32[]{:S(2)}, u32[]{:S(2)}) collective-permute-start(bf16[512,2,128]{2,0,1:T(8,128)(2,1)S(1)} %copy.29), channel_id=1, source_target_pairs={{0,16},{16,32},{32,48},{48,64},{64,80},{80,96},{96,112},{112,128},... | collective-permute-start | bytes 786440 | tf_op jit(solution)/shard_map/ppermute | solution.py:15
  58.5 0.0 all-to-all-done.1
  58.5 0.1 reshape.153
  58.6 52.4 %all_gather.6 = bf16[1024,2,128]{2,0,1:T(8,128)(2,1)S(1)} all-gather(bf16[32,2,128]{2,0,1:T(8,128)(2,1)S(1)} %bitcast.58), channel_id=1, replica_groups=mesh['ctx'=32,'head'=16] {'ctx'}, dimensions={0}, use_global_device_ids=true | all-gather | bytes 540672 | tf_op jit(solution)/shard_map/all_gather | solution.py:69
  111.1 37.2 %all_gather.7 = bf16[1024,2,128]{2,0,1:T(8,128)(2,1)S(1)} all-gather(bf16[32,2,128]{2,0,1:T(8,128)(2,1)S(1)} %bitcast.59), channel_id=1, replica_groups=mesh['ctx'=32,'head'=16] {'ctx'}, dimensions={0}, use_global_device_ids=true | all-gather | bytes 540672 | tf_op jit(solution)/shard_map/all_gather | solution.py:70
  148.2 1.1 fusion.3
  149.3 0.0 collective-permute-done
  149.3 0.0 collective-permute-done.1
  149.3 2.4 %fusion = (f32[2,512]{1,0:T(2,128)S(1)}, f32[2,1536,512]{2,1,0:T(8,128)S(1)}) fusion(pred[512,1536]{0,1:T(8,128)(4,1)S(1)} %fusion.7, bf16[512,2,128]{2,1,0:T(2,128)(2,1)S(1)} %reshape.153, bf16[512,2,128]{2,0,1:T(8,128)(2,1)S(1)} %copy.21, bf16[512,2,128]{2,0,1:T(8,128)(2,1)} %collective-permute-done.1, bf16[512,2,128]{2,0,1:T(8,128)(2,1)} %collective-permute-done), kind=kOutput, calls=%fused_computation.2 | convolution fusion | flops 409730048 | bytes 8130560 | tf_op jit(solution)/shard_map/qhd,khd->hqk/dot_general | solution.py:24
  151.8 1.7 fusion.1
  153.4 1.6 fusion.11
  155.0 1.5 fusion.9
  156.6 0.0 collective-permute-done.2
  156.6 0.0 collective-permute-done.3
  156.6 3.6 %fusion.23 = bf16[512,2,128]{2,0,1:T(8,128)(2,1)S(1)} fusion(f32[2,512,128]{2,1,0:T(8,128)S(1)} %fusion.11, f32[2,1536,512]{2,1,0:T(8,128)S(1)} %get-tuple-element.6, f32[2,512]{1,0:T(2,128)S(1)} %max.7, pred[512,1536]{0,1:T(8,128)(4,1)S(1)} %fusion.7, bf16[512,2,128]{2,0,1:T(8,128)(2,1)S(1)} %copy.29, bf16[512,2,128]{2,0,1:T(8,128)(2,1)} %collective-permute-done.3, ...), kind=kOutput, calls=%fused_computation.22 | convolution fusion | flops 413270016 | bytes 8658944 | tf_op jit(solution)/shard_map/hqk,khd->hqd/dot_general | solution.py:81
  160.2 0.3 copy.34
  160.4 0.2 all_to_all.59
  160.6 41.6 %all_to_all.67 = bf16[16,32,256]{2,1,0:T(8,128)(2,1)S(1)} all-to-all(bf16[16,32,256]{2,1,0:T(8,128)(2,1)S(1)} %all_to_all.59), channel_id=1, replica_groups=mesh['ctx'=32,'head'=16] {'head'}, dimensions={0} | all-to-all | bytes 524288 | tf_op jit(solution)/shard_map/all_to_all | solution.py:89
  202.2 0.7 copy.40
  (12 shorter events, 0.1 us)
Async XLA Ops:
  1.7 22.1 %all-to-all-start = ((bf16[32,16,256]{2,0,1:T(8,128)(2,1)}), bf16[32,16,256]{2,0,1:T(8,128)(2,1)S(1)}, u32[]{:S(2)}, u32[]{:S(2)}) async-start(bf16[32,16,256]{2,0,1:T(8,128)(2,1)} %bitcast.48), calls=%async_computation | async-start | bytes 524288 | tf_op jit(solution)/shard_map/all_to_all | solution.py:43
  23.7 14.5 %all-to-all-start.2 = ((bf16[32,16,256]{2,0,1:T(8,128)(2,1)}), bf16[32,16,256]{2,0,1:T(8,128)(2,1)S(1)}, u32[]{:S(2)}, u32[]{:S(2)}) async-start(bf16[32,16,256]{2,0,1:T(8,128)(2,1)} %bitcast.46), calls=%async_computation.2 | async-start | bytes 524288 | tf_op jit(solution)/shard_map/all_to_all | solution.py:44
  38.2 20.3 %all-to-all-start.1 = ((bf16[32,16,256]{2,0,1:T(8,128)(2,1)}), bf16[32,16,256]{2,0,1:T(8,128)(2,1)S(1)}, u32[]{:S(2)}, u32[]{:S(2)}) async-start(bf16[32,16,256]{2,0,1:T(8,128)(2,1)} %bitcast.47), calls=%async_computation.1 | async-start | bytes 524288 | tf_op jit(solution)/shard_map/all_to_all | solution.py:42
  43.0 106.3 %collective-permute-start = (bf16[512,2,128]{2,0,1:T(8,128)(2,1)S(1)}, bf16[512,2,128]{2,0,1:T(8,128)(2,1)}, u32[]{:S(2)}, u32[]{:S(2)}) collective-permute-start(bf16[512,2,128]{2,0,1:T(8,128)(2,1)S(1)} %copy.21), channel_id=1, source_target_pairs={{0,32},{16,48},{32,64},{48,80},{64,96},{80,112},{96,128},{112,144}... | collective-permute-start | bytes 786440 | tf_op jit(solution)/shard_map/ppermute | solution.py:15
  46.7 102.6 %collective-permute-start.1 = (bf16[512,2,128]{2,0,1:T(8,128)(2,1)S(1)}, bf16[512,2,128]{2,0,1:T(8,128)(2,1)}, u32[]{:S(2)}, u32[]{:S(2)}) collective-permute-start(bf16[512,2,128]{2,0,1:T(8,128)(2,1)S(1)} %copy.21), channel_id=1, source_target_pairs={{0,16},{16,32},{32,48},{48,64},{64,80},{80,96},{96,112},{112,128},... | collective-permute-start | bytes 786440 | tf_op jit(solution)/shard_map/ppermute | solution.py:15
  49.9 106.6 %collective-permute-start.2 = (bf16[512,2,128]{2,0,1:T(8,128)(2,1)S(1)}, bf16[512,2,128]{2,0,1:T(8,128)(2,1)}, u32[]{:S(2)}, u32[]{:S(2)}) collective-permute-start(bf16[512,2,128]{2,0,1:T(8,128)(2,1)S(1)} %copy.29), channel_id=1, source_target_pairs={{0,32},{16,48},{32,64},{48,80},{64,96},{80,112},{96,128},{112,144}... | collective-permute-start | bytes 786440 | tf_op jit(solution)/shard_map/ppermute | solution.py:15
  54.7 101.9 %collective-permute-start.3 = (bf16[512,2,128]{2,0,1:T(8,128)(2,1)S(1)}, bf16[512,2,128]{2,0,1:T(8,128)(2,1)}, u32[]{:S(2)}, u32[]{:S(2)}) collective-permute-start(bf16[512,2,128]{2,0,1:T(8,128)(2,1)S(1)} %copy.29), channel_id=1, source_target_pairs={{0,16},{16,32},{32,48},{48,64},{64,80},{80,96},{96,112},{112,128},... | collective-permute-start | bytes 786440 | tf_op jit(solution)/shard_map/ppermute | solution.py:15
where the time goes:
time: 204 us; the launch traced here: 203 us
  blocking collectives  131 us (64%)
  starting transfers between devices  32.3 us (16%)
  waiting for transfers between devices  19.1 us (9%)
  matrix products  8.69 us (4%)
  local copies, waits for them, and re-layouts  6.62 us (3%)
  other arithmetic  4.88 us (2%)
    all_gather x1, blocking collectives, local(): lax.all_gather(k_sum, 'ctx', axis=0, tiled=True)  52.4 us
    all_to_all x1, blocking collectives, local(): lax.all_to_all(local_out, 'head', split_axis=0, concat_axis=1, tiled=True)  41.6 us
    all_gather x1, blocking collectives, local(): lax.all_gather(v_sum, 'ctx', axis=0, tiled=True)  37.2 us
    ppermute x4, starting transfers between devices, from_behind(): lax.ppermute(value, axis, [(source, source + steps) for source in range(i...  15.3 us
    all_to_all x1, starting transfers between devices, local(): lax.all_to_all(keys, 'head', split_axis=1, concat_axis=0, tiled=True)  10.2 us
    all_to_all x1, waiting for transfers between devices, local(): lax.all_to_all(keys, 'head', split_axis=1, concat_axis=0, tiled=True)  10.2 us
    all_to_all x1, waiting for transfers between devices, local(): lax.all_to_all(values, 'head', split_axis=1, concat_axis=0, tiled=True)  8.91 us
  transfers between devices with their start and end apart: 7, of which 2 were waited for; matrix products, arithmetic and copies ran while one was open for 7% of the time, Pallas kernels for 0%

commit v1 on v0

--- a/solution.py
+++ b/solution.py
@@ -67,7 +67,9 @@
     query_rows = min(512, tok_rows)
     k_seen, v_seen = (
         lax.all_gather(k_sum, "ctx", axis=0, tiled=True),
-        lax.all_gather(v_sum, "ctx", axis=0, tiled=True),
+        jnp.concatenate(
+            lax.all_to_all(jnp.stack([v_sum] * lax.axis_size("ctx")), "ctx", 0, 0), axis=0
+        ),
     )
     spos = summary_positions(k_seen.shape[0])
     qpos = base + 0 + jnp.arange(query_rows, dtype=jnp.int32)

time: 204 us -> 171 us (0.84)
  blocking collectives: 131 us -> 84.1 us
  starting transfers between devices: 32.3 us -> 37.7 us
  waiting for transfers between devices: 19.1 us -> 24.5 us
  matrix products: 8.69 us -> 10.9 us
    all_gather x1 -> x0, blocking collectives: 37.2 us -> none  [local(): lax.all_gather(v_sum, 'ctx', axis=0, tiled=True)]
    all_to_all x1, blocking collectives: 41.6 us -> 31.7 us  [local(): lax.all_to_all(local_out, 'head', split_axis=0, concat_axis=1, tiled=True)]
    all_to_all x0 -> x1, starting transfers between devices: none -> 5.41 us  [local(): lax.all_to_all(jnp.stack([v_sum] * lax.axis_size('ctx')), 'ctx', 0, 0)]
    all_to_all x0 -> x1, waiting for transfers between devices: none -> 5.35 us  [local(): lax.all_to_all(jnp.stack([v_sum] * lax.axis_size('ctx')), 'ctx', 0, 0)]
  transfers between devices with their start and end apart: 7 -> 8, of which waited for: 2 -> 3; matrix products, arithmetic and copies ran while one was open for 7% -> 10% of each run, Pallas kernels for 0% -> 0%
where the time goes in v1:
time: 171 us; the launch traced here: 170 us
  blocking collectives  84.1 us (49%)
  starting transfers between devices  37.7 us (22%)
  waiting for transfers between devices  24.5 us (14%)
  matrix products  10.9 us (6%)
  local copies, waits for them, and re-layouts  8.19 us (5%)
  other arithmetic  4.85 us (3%)
    all_gather x1, blocking collectives, local(): lax.all_gather(k_sum, 'ctx', axis=0, tiled=True)  52.4 us
    all_to_all x1, blocking collectives, local(): lax.all_to_all(local_out, 'head', split_axis=0, concat_axis=1, tiled=True)  31.7 us
    ppermute x4, starting transfers between devices, from_behind(): lax.ppermute(value, axis, [(source, source + steps) for source in range(i...  15.2 us
    all_to_all x1, starting transfers between devices, local(): lax.all_to_all(keys, 'head', split_axis=1, concat_axis=0, tiled=True)  10.2 us
    all_to_all x1, waiting for transfers between devices, local(): lax.all_to_all(keys, 'head', split_axis=1, concat_axis=0, tiled=True)  10.2 us
    all_to_all x1, waiting for transfers between devices, local(): lax.all_to_all(values, 'head', split_axis=1, concat_axis=0, tiled=True)  8.91 us
    all_to_all x1, starting transfers between devices, local(): lax.all_to_all(jnp.stack([v_sum] * lax.axis_size('ctx')), 'ctx', 0, 0)  5.41 us
    all_to_all x1, waiting for transfers between devices, local(): lax.all_to_all(jnp.stack([v_sum] * lax.axis_size('ctx')), 'ctx', 0, 0)  5.35 us
  transfers between devices with their start and end apart: 8, of which 3 were waited for; matrix products, arithmetic and copies ran while one was open for 10% of the time, Pallas kernels for 0%

profile of v1, /device:TPU:1, one launch (start us, length us, event | category | flops | bytes accessed | tf_op | source)
XLA Modules:
  0.0 170.4 jit_solution(15636296580716383020)
XLA Ops:
  0.0 1.7 copy.71
  1.7 10.2 %all-to-all-start = ((bf16[32,16,256]{2,0,1:T(8,128)(2,1)}), bf16[32,16,256]{2,0,1:T(8,128)(2,1)S(1)}, u32[]{:S(2)}, u32[]{:S(2)}) async-start(bf16[32,16,256]{2,0,1:T(8,128)(2,1)} %bitcast.49), calls=%async_computation | async-start | bytes 524288 | tf_op jit(solution)/shard_map/all_to_all | solution.py:43
  11.9 1.7 copy.69
  13.6 10.2 %all-to-all-done = bf16[32,16,256]{2,0,1:T(8,128)(2,1)S(1)} async-done(((bf16[32,16,256]{2,0,1:T(8,128)(2,1)}), bf16[32,16,256]{2,0,1:T(8,128)(2,1)S(1)}, u32[]{:S(2)}, u32[]{:S(2)}) %all-to-all-start) | async-done | bytes 262176 | tf_op jit(solution)/shard_map/all_to_all | solution.py:43
  23.7 3.4 %all-to-all-start.2 = ((bf16[32,16,256]{2,0,1:T(8,128)(2,1)}), bf16[32,16,256]{2,0,1:T(8,128)(2,1)S(1)}, u32[]{:S(2)}, u32[]{:S(2)}) async-start(bf16[32,16,256]{2,0,1:T(8,128)(2,1)} %bitcast.47), calls=%async_computation.2 | async-start | bytes 524288 | tf_op jit(solution)/shard_map/all_to_all | solution.py:44
  27.2 1.7 copy.70
  28.9 0.4 subtract_compare_fusion.2
  29.3 8.9 %all-to-all-done.2 = bf16[32,16,256]{2,0,1:T(8,128)(2,1)S(1)} async-done(((bf16[32,16,256]{2,0,1:T(8,128)(2,1)}), bf16[32,16,256]{2,0,1:T(8,128)(2,1)S(1)}, u32[]{:S(2)}, u32[]{:S(2)}) %all-to-all-start.2) | async-done | bytes 262176 | tf_op jit(solution)/shard_map/all_to_all | solution.py:44
  38.2 3.4 %all-to-all-start.1 = ((bf16[32,16,256]{2,0,1:T(8,128)(2,1)}), bf16[32,16,256]{2,0,1:T(8,128)(2,1)S(1)}, u32[]{:S(2)}, u32[]{:S(2)}) async-start(bf16[32,16,256]{2,0,1:T(8,128)(2,1)} %bitcast.48), calls=%async_computation.1 | async-start | bytes 524288 | tf_op jit(solution)/shard_map/all_to_all | solution.py:42
  41.6 1.3 fusion.7
  42.9 0.1 reshape.154
  43.0 3.7 %collective-permute-start = (bf16[512,2,128]{2,0,1:T(8,128)(2,1)S(1)}, bf16[512,2,128]{2,0,1:T(8,128)(2,1)}, u32[]{:S(2)}, u32[]{:S(2)}) collective-permute-start(bf16[512,2,128]{2,0,1:T(8,128)(2,1)S(1)} %copy.37), channel_id=1, source_target_pairs={{0,32},{16,48},{32,64},{48,80},{64,96},{80,112},{96,128},{112,144}... | collective-permute-start | bytes 786440 | tf_op jit(solution)/shard_map/ppermute | solution.py:15
  46.7 2.9 %collective-permute-start.1 = (bf16[512,2,128]{2,0,1:T(8,128)(2,1)S(1)}, bf16[512,2,128]{2,0,1:T(8,128)(2,1)}, u32[]{:S(2)}, u32[]{:S(2)}) collective-permute-start(bf16[512,2,128]{2,0,1:T(8,128)(2,1)S(1)} %copy.37), channel_id=1, source_target_pairs={{0,16},{16,32},{32,48},{48,64},{64,80},{80,96},{96,112},{112,128},... | collective-permute-start | bytes 786440 | tf_op jit(solution)/shard_map/ppermute | solution.py:15
  49.7 0.1 reshape_reshape.6
  49.7 0.1 reshape_reshape.7
  49.8 0.1 reshape.157
  49.9 4.8 %collective-permute-start.2 = (bf16[512,2,128]{2,0,1:T(8,128)(2,1)S(1)}, bf16[512,2,128]{2,0,1:T(8,128)(2,1)}, u32[]{:S(2)}, u32[]{:S(2)}) collective-permute-start(bf16[512,2,128]{2,0,1:T(8,128)(2,1)S(1)} %copy.45), channel_id=1, source_target_pairs={{0,32},{16,48},{32,64},{48,80},{64,96},{80,112},{96,128},{112,144}... | collective-permute-start | bytes 786440 | tf_op jit(solution)/shard_map/ppermute | solution.py:15
  54.7 3.8 %collective-permute-start.3 = (bf16[512,2,128]{2,0,1:T(8,128)(2,1)S(1)}, bf16[512,2,128]{2,0,1:T(8,128)(2,1)}, u32[]{:S(2)}, u32[]{:S(2)}) collective-permute-start(bf16[512,2,128]{2,0,1:T(8,128)(2,1)S(1)} %copy.45), channel_id=1, source_target_pairs={{0,16},{16,32},{32,48},{48,64},{64,80},{80,96},{96,112},{112,128},... | collective-permute-start | bytes 786440 | tf_op jit(solution)/shard_map/ppermute | solution.py:15
  58.5 0.0 all-to-all-done.1
  58.5 0.1 reshape.155
  58.6 52.4 %all_gather.3 = bf16[1024,2,128]{2,0,1:T(8,128)(2,1)S(1)} all-gather(bf16[32,2,128]{2,0,1:T(8,128)(2,1)S(1)} %bitcast.60), channel_id=1, replica_groups=mesh['ctx'=32,'head'=16] {'ctx'}, dimensions={0}, use_global_device_ids=true | all-gather | bytes 540672 | tf_op jit(solution)/shard_map/all_gather | solution.py:69
  111.1 0.9 stack.3
  112.0 5.4 %all-to-all-start.3 = ((bf16[32,32,2,128]{3,1,2,0:T(8,128)(2,1)}), bf16[32,32,2,128]{3,1,2,0:T(8,128)(2,1)S(1)}, u32[]{:S(2)}, u32[]{:S(2)}) async-start(bf16[32,32,2,128]{3,1,2,0:T(8,128)(2,1)} %stack.3), calls=%async_computation.3 | async-start | bytes 1048576 | tf_op jit(solution)/shard_map/all_to_all | solution.py:71
  117.4 1.1 fusion.3
  118.5 0.0 copy-start.2
  118.5 0.0 collective-permute-done
  118.5 0.0 collective-permute-done.1
  118.5 2.8 %fusion = (f32[2,512]{1,0:T(2,128)S(1)}, f32[2,1536,512]{2,1,0:T(8,128)S(1)}) fusion(pred[512,1536]{0,1:T(8,128)(4,1)S(1)} %fusion.7, bf16[512,2,128]{2,1,0:T(2,128)(2,1)S(1)} %reshape.155, bf16[512,2,128]{2,0,1:T(8,128)(2,1)S(1)} %copy.37, bf16[512,2,128]{2,0,1:T(8,128)(2,1)} %collective-permute-done.1, bf16[512,2,128]{2,0,1:T(8,128)(2,1)} %collective-permute-done), kind=kOutput, calls=%fused_computation.2 | convolution fusion | flops 409730048 | bytes 8130560 | tf_op jit(solution)/shard_map/qhd,khd->hqk/dot_general | solution.py:24
  121.3 0.0 copy-start
  121.4 0.0 copy-done.2
  121.4 1.5 fusion.9
  122.8 1.7 fusion.1
  124.5 0.0 copy-done
  124.6 5.3 %all-to-all-done.3 = bf16[32,32,2,128]{3,1,2,0:T(8,128)(2,1)S(1)} async-done(((bf16[32,32,2,128]{3,1,2,0:T(8,128)(2,1)}), bf16[32,32,2,128]{3,1,2,0:T(8,128)(2,1)S(1)}, u32[]{:S(2)}, u32[]{:S(2)}) %all-to-all-start.3) | async-done | bytes 524320 | tf_op jit(solution)/shard_map/all_to_all | solution.py:71
  129.9 0.0 copy-start.1
  130.0 3.4 %fusion.11 = f32[2,512,128]{2,1,0:T(8,128)S(1)} fusion(bf16[1024,2,128]{2,0,1:T(8,128)(2,1)S(1)} %bitcast.56, f32[2,512,1024]{2,1,0:T(8,128)} %copy-done.2, f32[2,512]{1,0:T(2,128)S(1)} %max.7, pred[512,1024]{1,0:T(8,128)(4,1)S(1)} %subtract_compare_fusion.2), kind=kOutput, calls=%fused_computation.17 | convolution fusion | flops 273678336 | bytes 5771264 | tf_op jit(solution)/shard_map/hqk,khd->hqd/dot_general | solution.py:86
  133.4 0.0 collective-permute-done.2
  133.4 0.0 collective-permute-done.3
  133.4 0.6 copy-done.1
  134.0 3.6 %fusion.23 = bf16[512,2,128]{2,0,1:T(8,128)(2,1)S(1)} fusion(f32[2,512,128]{2,1,0:T(8,128)S(1)} %fusion.11, f32[2,1536,512]{2,1,0:T(8,128)S(1)} %copy-done.1, f32[2,512]{1,0:T(2,128)S(1)} %max.7, pred[512,1536]{0,1:T(8,128)(4,1)S(1)} %fusion.7, bf16[512,2,128]{2,0,1:T(8,128)(2,1)S(1)} %copy.45, bf16[512,2,128]{2,0,1:T(8,128)(2,1)} %collective-permute-done.3, ...), kind=kOutput, calls=%fused_computation.22 | convolution fusion | flops 413270016 | bytes 8658944 | tf_op jit(solution)/shard_map/hqk,khd->hqd/dot_general | solution.py:83
  137.6 0.3 copy.51
  137.8 0.2 all_to_all.63
  138.0 31.7 %all_to_all.72 = bf16[16,32,256]{2,1,0:T(8,128)(2,1)S(1)} all-to-all(bf16[16,32,256]{2,1,0:T(8,128)(2,1)S(1)} %all_to_all.63), channel_id=1, replica_groups=mesh['ctx'=32,'head'=16] {'head'}, dimensions={0} | all-to-all | bytes 524288 | tf_op jit(solution)/shard_map/all_to_all | solution.py:91
  169.7 0.7 copy.57
  (13 shorter events, 0.2 us)
Async XLA Ops:
  1.7 22.1 %all-to-all-start = ((bf16[32,16,256]{2,0,1:T(8,128)(2,1)}), bf16[32,16,256]{2,0,1:T(8,128)(2,1)S(1)}, u32[]{:S(2)}, u32[]{:S(2)}) async-start(bf16[32,16,256]{2,0,1:T(8,128)(2,1)} %bitcast.49), calls=%async_computation | async-start | bytes 524288 | tf_op jit(solution)/shard_map/all_to_all | solution.py:43
  23.7 14.5 %all-to-all-start.2 = ((bf16[32,16,256]{2,0,1:T(8,128)(2,1)}), bf16[32,16,256]{2,0,1:T(8,128)(2,1)S(1)}, u32[]{:S(2)}, u32[]{:S(2)}) async-start(bf16[32,16,256]{2,0,1:T(8,128)(2,1)} %bitcast.47), calls=%async_computation.2 | async-start | bytes 524288 | tf_op jit(solution)/shard_map/all_to_all | solution.py:44
  38.2 20.3 %all-to-all-start.1 = ((bf16[32,16,256]{2,0,1:T(8,128)(2,1)}), bf16[32,16,256]{2,0,1:T(8,128)(2,1)S(1)}, u32[]{:S(2)}, u32[]{:S(2)}) async-start(bf16[32,16,256]{2,0,1:T(8,128)(2,1)} %bitcast.48), calls=%async_computation.1 | async-start | bytes 524288 | tf_op jit(solution)/shard_map/all_to_all | solution.py:42
  43.0 75.5 %collective-permute-start = (bf16[512,2,128]{2,0,1:T(8,128)(2,1)S(1)}, bf16[512,2,128]{2,0,1:T(8,128)(2,1)}, u32[]{:S(2)}, u32[]{:S(2)}) collective-permute-start(bf16[512,2,128]{2,0,1:T(8,128)(2,1)S(1)} %copy.37), channel_id=1, source_target_pairs={{0,32},{16,48},{32,64},{48,80},{64,96},{80,112},{96,128},{112,144}... | collective-permute-start | bytes 786440 | tf_op jit(solution)/shard_map/ppermute | solution.py:15
  46.7 71.8 %collective-permute-start.1 = (bf16[512,2,128]{2,0,1:T(8,128)(2,1)S(1)}, bf16[512,2,128]{2,0,1:T(8,128)(2,1)}, u32[]{:S(2)}, u32[]{:S(2)}) collective-permute-start(bf16[512,2,128]{2,0,1:T(8,128)(2,1)S(1)} %copy.37), channel_id=1, source_target_pairs={{0,16},{16,32},{32,48},{48,64},{64,80},{80,96},{96,112},{112,128},... | collective-permute-start | bytes 786440 | tf_op jit(solution)/shard_map/ppermute | solution.py:15
  49.9 83.5 %collective-permute-start.2 = (bf16[512,2,128]{2,0,1:T(8,128)(2,1)S(1)}, bf16[512,2,128]{2,0,1:T(8,128)(2,1)}, u32[]{:S(2)}, u32[]{:S(2)}) collective-permute-start(bf16[512,2,128]{2,0,1:T(8,128)(2,1)S(1)} %copy.45), channel_id=1, source_target_pairs={{0,32},{16,48},{32,64},{48,80},{64,96},{80,112},{96,128},{112,144}... | collective-permute-start | bytes 786440 | tf_op jit(solution)/shard_map/ppermute | solution.py:15
  54.7 78.7 %collective-permute-start.3 = (bf16[512,2,128]{2,0,1:T(8,128)(2,1)S(1)}, bf16[512,2,128]{2,0,1:T(8,128)(2,1)}, u32[]{:S(2)}, u32[]{:S(2)}) collective-permute-start(bf16[512,2,128]{2,0,1:T(8,128)(2,1)S(1)} %copy.45), channel_id=1, source_target_pairs={{0,16},{16,32},{32,48},{48,64},{64,80},{80,96},{96,112},{112,128},... | collective-permute-start | bytes 786440 | tf_op jit(solution)/shard_map/ppermute | solution.py:15
  112.0 17.9 %all-to-all-start.3 = ((bf16[32,32,2,128]{3,1,2,0:T(8,128)(2,1)}), bf16[32,32,2,128]{3,1,2,0:T(8,128)(2,1)S(1)}, u32[]{:S(2)}, u32[]{:S(2)}) async-start(bf16[32,32,2,128]{3,1,2,0:T(8,128)(2,1)} %stack.3), calls=%async_computation.3 | async-start | bytes 1048576 | tf_op jit(solution)/shard_map/all_to_all | solution.py:71
  118.5 2.9 %copy-start.2 = (f32[2,512,1024]{2,1,0:T(8,128)}, f32[2,512,1024]{2,1,0:T(8,128)S(1)}, u32[]{:S(2)}) copy-start(f32[2,512,1024]{2,1,0:T(8,128)S(1)} %get-tuple-element.8) | copy-start | bytes 12582916
  121.3 3.2 %copy-start = (f32[2,1536,512]{2,1,0:T(8,128)}, f32[2,1536,512]{2,1,0:T(8,128)S(1)}, u32[]{:S(2)}) copy-start(f32[2,1536,512]{2,1,0:T(8,128)S(1)} %get-tuple-element.6) | copy-start | bytes 18874372
  129.9 4.0 %copy-start.1 = (f32[2,1536,512]{2,1,0:T(8,128)S(1)}, f32[2,1536,512]{2,1,0:T(8,128)}, u32[]{:S(2)}) copy-start(f32[2,1536,512]{2,1,0:T(8,128)} %copy-done) | copy-start | bytes 18874372
